TPU v7x, 32 devices: a whole 2x2x4 slice. The times are simulated.
32 devices in a mesh: dp: 4 (over y, x), seq: 8 (over z, core).
Axes of the slice: x: 2, y: 2, z: 4, core: 2. Of those that a mesh axis runs over, the one named last changes fastest.
Arguments:
- tokens: float32 [4, 1024, 1024], P('dp', 'seq'), may hold values from -6 to 6
- cotangent: float32 [4, 1024, 1024], P('dp', 'seq'), may hold values from -6 to 6
- doc_ids: int32 [4, 1024], P('dp'), may hold values from 0 to 1, never falling along the last dimension, each value on 1 to 768 neighbouring positions
- in_weight: float32 [1024, 4384], P(('dp', 'seq')), may hold values from -0.1875 to 0.1875
- out_weight: float32 [1024, 2048], P(('dp', 'seq')), may hold values from -0.125 to 0.125
- in_m: float32 [1024, 4384], P(('dp', 'seq')), may hold values from -30 to 30
- in_v: float32 [1024, 4384], P(('dp', 'seq')), may hold values from 1 to 1000
- out_m: float32 [1024, 2048], P(('dp', 'seq')), may hold values from -30 to 30
- out_v: float32 [1024, 2048], P(('dp', 'seq')), may hold values from 1 to 1000
- vec_params: float32 [14688], replicated, as said below
- vec_m: float32 [14688], replicated, may hold values from -30 to 30
- vec_v: float32 [14688], replicated, may hold values from 1 to 1000
Outputs:
- activations: float32 [4, 1024, 1024], P('dp', 'seq')
- input_grad: float32 [4, 1024, 1024], P('dp', 'seq')
- in_grad: float32 [1024, 4384], P(('dp', 'seq'))
- out_grad: float32 [1024, 2048], P(('dp', 'seq'))
- vec_grad: float32 [14688], replicated
- in_new: float32 [1024, 4384], P(('dp', 'seq'))
- out_new: float32 [1024, 2048], P(('dp', 'seq'))
- vec_new: float32 [14688], replicated
- in_m_new: float32 [1024, 4384], P(('dp', 'seq'))
- in_v_new: float32 [1024, 4384], P(('dp', 'seq'))
- out_m_new: float32 [1024, 2048], P(('dp', 'seq'))
- out_v_new: float32 [1024, 2048], P(('dp', 'seq'))
- vec_m_new: float32 [14688], replicated
- vec_v_new: float32 [14688], replicated
Inputs may be any that keep to these rules, and one draw needn't show every extreme that they name: `doc_ids`: each row holds document 0 and then document 1, each of one or more positions, none longer than 768. `vec_params`: norm_gain and gate_gain lie in 0.7 to 1.3, skip_gain in 0.5 to 1.5, step_bias in -1 to 1, log_rate in -12 to -3.
All inputs are finite; a program needn't handle non-finite values.
Results may differ from a plain program's by a relative error of at most 0.015.
Values may be sent and summed in bfloat16 or wider, within the bound.
A program may use at most 192 MiB of HBM per device.

v0:
```python
import jax
import jax.numpy as jnp
from jax import lax
from jax.sharding import PartitionSpec as P

D = 1024
DI = 2048
H = 32
P_SIZE = 64
N = 128
KW = 4
STRETCH = 256
STEP = 10
CONV = 2304
norm_eps = 1e-05
beta_one = 0.9
beta_two = 0.95
learn_rate = 0.03
decay_rate = 0.1
adam_eps = 1e-08
top_precision = lax.Precision.HIGHEST


def shifted_2(block, axis, distance):
    devices = range(lax.axis_size(axis))
    route = [(i - distance, i) for i in devices if i - distance in devices]
    return lax.ppermute(block, axis, route)


def unpack(vector):
    cursor = D + DI
    norm_gain = vector[:D]
    gate_gain = vector[D:cursor]
    conv_kernel = vector[cursor : cursor + KW * CONV].reshape(KW, CONV)
    cursor = cursor + KW * CONV
    conv_bias = vector[cursor : cursor + CONV]
    cursor = cursor + CONV
    step_bias = vector[cursor : cursor + H]
    log_rate = vector[cursor + H : cursor + 2 * H]
    skip_gain = vector[cursor + 2 * H : cursor + 3 * H]
    return (norm_gain, gate_gain, conv_kernel, conv_bias, step_bias, log_rate, skip_gain)


def repack(norm_gain, gate_gain, conv_kernel, conv_bias, step_bias, log_rate, skip_gain):
    return jnp.concatenate(
        [norm_gain, gate_gain, conv_kernel.reshape(-1), conv_bias, step_bias, log_rate, skip_gain]
    )


def input_norm(inputs, gain):
    scale = lax.rsqrt(jnp.mean(inputs * inputs, axis=-1, keepdims=True) + norm_eps)
    return inputs * scale * gain[None, :]


def gate_norm(ssd_out, gate_in, gain):
    mixed = ssd_out * jax.nn.silu(gate_in)
    scale = lax.rsqrt(jnp.mean(mixed * mixed, axis=-1, keepdims=True) + norm_eps)
    return mixed * scale * gain[None, :]


def conv_silu(padded, conv_kernel, conv_bias, ext_ids):
    length = padded.shape[0] - (KW - 1)
    own_ids = ext_ids[KW - 1 :]
    total = jnp.zeros((length, padded.shape[1]), jnp.float32) + conv_bias[None, :]
    for offset in range(KW):
        valid = (ext_ids[offset : offset + length] == own_ids).astype(jnp.float32)
        total = (
            total + conv_kernel[offset][None, :] * padded[offset : offset + length] * valid[:, None]
        )
    return jax.nn.silu(total)


def rates(step_raw, step_bias, log_rate):
    step_size = jax.nn.softplus(step_raw + step_bias[None, :])
    log_decay = -jnp.exp(log_rate)[None, :] * step_size
    return (step_size, log_decay)


def ssd_block(state, pieces):
    values, input_map, output_map, step_size, log_decay, block_ids, prior_id = pieces
    length = values.shape[0]
    cumulative = jnp.cumsum(log_decay, axis=0)
    rows_index = lax.broadcasted_iota(jnp.int32, (length, length), 0)
    cols_index = lax.broadcasted_iota(jnp.int32, (length, length), 1)
    related = (block_ids[:, None] == block_ids[None, :]) & (rows_index >= cols_index)
    spans = cumulative.T[:, :, None] - cumulative.T[:, None, :]
    decays = jnp.where(related[None], jnp.exp(jnp.where(related[None], spans, 0.0)), 0.0)
    scores = jnp.dot(output_map, input_map.T, precision=top_precision)
    mixing = decays * scores[None] * step_size.T[:, None, :]
    inside = jnp.einsum("hij,jhp->ihp", mixing, values, precision=top_precision)
    carried = (block_ids == prior_id).astype(jnp.float32)
    reach = carried[:, None] * jnp.exp(cumulative)
    entering = (
        jnp.einsum("hpn,in->ihp", state, output_map, precision=top_precision) * reach[:, :, None]
    )
    ending = (block_ids == block_ids[-1]).astype(jnp.float32)
    tail_weight = ending[:, None] * jnp.exp(cumulative[-1][None, :] - cumulative) * step_size
    new_state = state * reach[-1][:, None, None] + jnp.einsum(
        "jh,jhp,jn->hpn", tail_weight, values, input_map, precision=top_precision
    )
    return (new_state, inside + entering)


def ssd_run(mixed_in, step_size, log_decay, skip_gain, row_ids, prior_id, state, block):
    length = mixed_in.shape[0]
    blocks = length // block
    values = mixed_in[:, :DI].reshape(length, H, P_SIZE)
    input_map = mixed_in[:, DI : DI + N]
    output_map = mixed_in[:, DI + N :]
    shifted = jnp.concatenate([jnp.reshape(prior_id, (1,)), row_ids[:-1]])
    priors = shifted.reshape(blocks, block)[:, 0]
    pieces = (
        values.reshape(blocks, block, H, P_SIZE),
        input_map.reshape(blocks, block, N),
        output_map.reshape(blocks, block, N),
        step_size.reshape(blocks, block, H),
        log_decay.reshape(blocks, block, H),
        row_ids.reshape(blocks, block),
        priors,
    )
    final, outputs = lax.scan(ssd_block, state, pieces)
    result = outputs.reshape(length, H, P_SIZE) + skip_gain[None, :, None] * values
    return (result.reshape(length, DI), final)


def adamw_update(param, grad, first, second):
    first_new = beta_one * first + (1.0 - beta_one) * grad
    second_new = beta_two * second + (1.0 - beta_two) * grad * grad
    corrected = first_new / (1.0 - beta_one**STEP)
    scaled = jnp.sqrt(second_new / (1.0 - beta_two**STEP)) + adam_eps
    return (
        param * (1.0 - learn_rate * decay_rate) - learn_rate * corrected / scaled,
        first_new,
        second_new,
    )


def body(
    tokens,
    cotangent,
    doc_ids,
    in_weight,
    out_weight,
    in_m,
    in_v,
    out_m,
    out_v,
    vec_params,
    vec_m,
    vec_v,
):
    in_work, out_work = (
        lax.all_gather(in_weight.astype(jnp.bfloat16), ("dp", "seq"), axis=0, tiled=True),
        lax.all_gather(out_weight.astype(jnp.bfloat16), ("dp", "seq"), axis=0, tiled=True),
    )
    norm_gain, gate_gain, conv_kernel, conv_bias, step_bias, log_rate, skip_gain = unpack(
        vec_params
    )
    inputs = tokens[0]
    upstream_f = cotangent[0]
    local_len = inputs.shape[0]
    block = min(STRETCH, local_len)
    padded_row = jnp.concatenate([jnp.full((KW - 1,), -1, jnp.int32), doc_ids[0]])
    offset = lax.axis_index("seq") * local_len
    ext_ids = lax.dynamic_slice_in_dim(padded_row, offset, local_len + KW - 1)
    own_ids = ext_ids[KW - 1 :]
    prior_id = ext_ids[KW - 2]
    zero_state = jnp.zeros((H, P_SIZE, N), jnp.float32)
    normed = input_norm(inputs, norm_gain).astype(jnp.bfloat16)
    projected = jnp.dot(normed, in_work, preferred_element_type=jnp.float32)
    gate_in = projected[:, :DI]
    conv_in = projected[:, DI : DI + CONV].astype(jnp.bfloat16)
    step_raw = projected[:, DI + CONV :]
    rim = shifted_2(conv_in[local_len - (KW - 1) :], "seq", 1)
    padded = lax.optimization_barrier(jnp.concatenate([rim, conv_in], axis=0)).astype(jnp.float32)
    mixed_in = lax.optimization_barrier(
        conv_silu(padded, conv_kernel, conv_bias, ext_ids).astype(jnp.bfloat16)
    ).astype(jnp.float32)
    output_map = mixed_in[:, DI + N :]

    def pre_chain(mixed, raw, bias_in, rate_in, skip_in):
        step_size, log_decay = rates(raw, bias_in, rate_in)
        local_out, local_state = ssd_run(
            mixed, step_size, log_decay, skip_in, own_ids, prior_id, zero_state, block
        )
        cumulative = jnp.cumsum(log_decay, axis=0)
        reach = (own_ids == prior_id).astype(jnp.float32)[:, None] * jnp.exp(cumulative)
        return (local_out, local_state, reach)

    local_out, local_state, reach = pre_chain(mixed_in, step_raw, step_bias, log_rate, skip_gain)
    decay = reach[-1]

    def relay(turn, entry_now):
        return shifted_2(decay[:, None, None] * entry_now + local_state, "seq", 1)

    entry = lax.fori_loop(0, lax.axis_size("seq") - 1, relay, zero_state)
    entering = (
        jnp.einsum("hpn,tn->thp", entry, output_map, precision=top_precision) * reach[:, :, None]
    )
    ssd_out = local_out + entering.reshape(local_len, DI)
    gated, gate_back = jax.vjp(gate_norm, ssd_out, gate_in, gate_gain)
    normed_out = gated.astype(jnp.bfloat16)
    outputs = inputs + lax.dot_general(
        normed_out, out_work, (((1,), (1,)), ((), ())), preferred_element_type=jnp.float32
    )
    upstream = upstream_f.astype(jnp.bfloat16)
    grad_gated = jnp.dot(upstream, out_work, preferred_element_type=jnp.float32)
    grad_ssd, grad_gate_in, grad_gate_gain = gate_back(grad_gated)
    own_part = jnp.einsum(
        "th,thp,tn->hpn",
        reach,
        grad_ssd.reshape(local_len, H, P_SIZE),
        output_map,
        precision=top_precision,
    )

    def back_relay(turn, later):
        return shifted_2(
            (own_part + decay[:, None, None] * later).astype(jnp.bfloat16), "seq", -1
        ).astype(jnp.float32)

    after = lax.fori_loop(0, lax.axis_size("seq") - 1, back_relay, zero_state)

    def complete(mixed, raw, bias_in, rate_in, skip_in):
        part_out, part_state, part_reach = pre_chain(mixed, raw, bias_in, rate_in, skip_in)
        reader = mixed[:, DI + N :]
        arriving = (
            jnp.einsum("hpn,tn->thp", entry, reader, precision=top_precision)
            * part_reach[:, :, None]
        )
        return (part_out + arriving.reshape(local_len, DI), part_reach[-1], part_state)

    _, ssd_back = jax.vjp(complete, mixed_in, step_raw, step_bias, log_rate, skip_gain)
    grad_mixed, grad_raw, grad_bias, grad_rate, grad_skip = ssd_back(
        (grad_ssd, jnp.sum(after * entry, axis=(1, 2)), after)
    )
    _, conv_back = jax.vjp(
        lambda values, kernel, constant: conv_silu(values, kernel, constant, ext_ids),
        padded,
        conv_kernel,
        conv_bias,
    )
    grad_padded, grad_kernel, grad_cbias = conv_back(grad_mixed)
    returned = shifted_2(grad_padded[: KW - 1], "seq", -1)
    grad_conv = jnp.concatenate(
        [grad_padded[KW - 1 : local_len], grad_padded[local_len:] + returned], axis=0
    )
    grad_proj = jnp.concatenate([grad_gate_in, grad_conv, grad_raw], axis=1).astype(jnp.bfloat16)
    grad_normed = lax.dot_general(
        grad_proj, in_work, (((1,), (1,)), ((), ())), preferred_element_type=jnp.float32
    )
    _, norm_back = jax.vjp(input_norm, inputs, norm_gain)
    grad_inputs, grad_norm_gain = norm_back(grad_normed)
    vector = repack(
        grad_norm_gain, grad_gate_gain, grad_kernel, grad_cbias, grad_bias, grad_rate, grad_skip
    )
    dp_count = lax.axis_size("dp")
    seq_count = lax.axis_size("seq")
    owner_rows = in_weight.shape[0]
    seq_place = lax.axis_index("seq")

    def select_rows(matrix):
        count = matrix.shape[0]
        grouped = matrix.reshape(count, dp_count, seq_count, owner_rows)
        chosen = lax.dynamic_slice_in_dim(grouped, seq_place, 1, 2)
        return chosen.reshape(count, dp_count * owner_rows)

    normed_piece = lax.all_gather(normed, "seq", axis=0, tiled=True)
    proj_piece = lax.all_gather(grad_proj, "seq", axis=0, tiled=True)
    upstream_piece = lax.all_gather(upstream, "seq", axis=0, tiled=True)
    out_piece = lax.all_gather(normed_out, "seq", axis=0, tiled=True)
    first = lax.dot_general(
        select_rows(normed_piece),
        proj_piece,
        (((0,), (0,)), ((), ())),
        preferred_element_type=jnp.float32,
    )
    second = lax.dot_general(
        select_rows(upstream_piece),
        out_piece,
        (((0,), (0,)), ((), ())),
        preferred_element_type=jnp.float32,
    )
    in_part, out_part = (
        lax.psum_scatter(
            first.reshape(dp_count, owner_rows, grad_proj.shape[1]).astype(jnp.bfloat16),
            "dp",
            scatter_dimension=0,
            tiled=True,
        ).astype(jnp.float32),
        lax.psum_scatter(
            second.reshape(dp_count, owner_rows, normed_out.shape[1]).astype(jnp.bfloat16),
            "dp",
            scatter_dimension=0,
            tiled=True,
        ).astype(jnp.float32),
    )
    in_grad = in_part.reshape(owner_rows, grad_proj.shape[1])
    out_grad = out_part.reshape(owner_rows, normed_out.shape[1])
    vec_grad = lax.psum(vector, ("dp", "seq"))
    in_new, in_m_new, in_v_new = adamw_update(in_weight, in_grad, in_m, in_v)
    out_new, out_m_new, out_v_new = adamw_update(out_weight, out_grad, out_m, out_v)
    vec_new, vec_m_new, vec_v_new = adamw_update(vec_params, vec_grad, vec_m, vec_v)
    return (
        outputs[None],
        (upstream_f + grad_inputs)[None],
        in_grad,
        out_grad,
        vec_grad,
        in_new,
        out_new,
        vec_new,
        in_m_new,
        in_v_new,
        out_m_new,
        out_v_new,
        vec_m_new,
        vec_v_new,
    )


def solution(mesh):
    in_specs = (
        P("dp", "seq", None),
        P("dp", "seq", None),
        P("dp", None),
        P(("dp", "seq"), None),
        P(("dp", "seq"), None),
        P(("dp", "seq"), None),
        P(("dp", "seq"), None),
        P(("dp", "seq"), None),
        P(("dp", "seq"), None),
        P(),
        P(),
        P(),
    )
    out_specs = (
        P("dp", "seq", None),
        P("dp", "seq", None),
        P(("dp", "seq"), None),
        P(("dp", "seq"), None),
        P(),
        P(("dp", "seq"), None),
        P(("dp", "seq"), None),
        P(),
        P(("dp", "seq"), None),
        P(("dp", "seq"), None),
        P(("dp", "seq"), None),
        P(("dp", "seq"), None),
        P(),
        P(),
    )
    return jax.shard_map(body, mesh=mesh, in_specs=in_specs, out_specs=out_specs, check_vma=False)
```

profile of v0, /device:TPU:0, one launch (start us, length us, event | category | flops | bytes accessed | tf_op | source)
XLA Modules:
  0.0 678.0 jit_solution(5091734478298455227)
XLA Ops:
  15.3 2.6 compare_convert_fusion
  17.9 76.6 %all-gather.7.cloned.1.call-done = bf16[1024,4384]{1,0:T(8,128)(2,1)} async-done(((bf16[32,4384]{1,0:T(8,128)(2,1)}), bf16[1024,4384]{1,0:T(8,128)(2,1)}) %all-gather.7.cloned.1.call-update) | async-done | bytes 8978448 | tf_op jit(solution)/shard_map/all_gather | solution.py:153
  94.5 5.1 fusion.124
  101.3 2.7 collective-permute-start.2
  115.6 2.6 copy.208
  125.2 2.7 convolution_add_fusion
  128.1 152.6 %while.7 = (s32[]{:T(128)}, f32[32,64,128]{2,1,0:T(8,128)S(1)}, f32[1,32]{1,0:T(1,128)S(1)}, f32[32,64,128]{2,1,0:T(8,128)}, s32[]{:T(128)}) while((s32[]{:T(128)}, f32[32,64,128]{2,1,0:T(8,128)S(1)}, f32[1,32]{1,0:T(1,128)S(1)}, f32[32,64,128]{2,1,0:T(8,128)}, s32[]{:T(128)}) %tuple.149), condition=%wide.region_3.4_spmd, body=%wide.region_2.3_spmd.sunk | while | flops 524290 | bytes 7340261 | solution.py:196
  128.5 2.4 multiply_add_fusion.13
  130.9 2.6 collective-permute-start
  133.5 2.4 collective-permute-done
  136.0 2.4 multiply_add_fusion.13
  138.4 23.1 %collective-permute-start = (f32[32,64,128]{2,1,0:T(8,128)}, f32[32,64,128]{2,1,0:T(8,128)S(1)}, u32[]{:S(2)}, u32[]{:S(2)}) collective-permute-start(f32[32,64,128]{2,1,0:T(8,128)} %multiply_add_fusion.13), channel_id=1, source_target_pairs={{0,1},{1,2},{2,3},{3,4},{4,5},{5,6},{6,7},{8,9},{9,10},{10,11},{11... | collective-permute-start | bytes 3145736 | tf_op jit(solution)/shard_map/while/body/eval_jaxpr/ppermute | solution.py:27
  161.5 2.4 collective-permute-done
  163.9 2.4 multiply_add_fusion.13
  166.3 27.7 %collective-permute-start = (f32[32,64,128]{2,1,0:T(8,128)}, f32[32,64,128]{2,1,0:T(8,128)S(1)}, u32[]{:S(2)}, u32[]{:S(2)}) collective-permute-start(f32[32,64,128]{2,1,0:T(8,128)} %multiply_add_fusion.13), channel_id=1, source_target_pairs={{0,1},{1,2},{2,3},{3,4},{4,5},{5,6},{6,7},{8,9},{9,10},{10,11},{11... | collective-permute-start | bytes 3145736 | tf_op jit(solution)/shard_map/while/body/eval_jaxpr/ppermute | solution.py:27
  194.0 2.4 collective-permute-done
  196.4 2.4 multiply_add_fusion.13
  198.8 22.8 %collective-permute-start = (f32[32,64,128]{2,1,0:T(8,128)}, f32[32,64,128]{2,1,0:T(8,128)S(1)}, u32[]{:S(2)}, u32[]{:S(2)}) collective-permute-start(f32[32,64,128]{2,1,0:T(8,128)} %multiply_add_fusion.13), channel_id=1, source_target_pairs={{0,1},{1,2},{2,3},{3,4},{4,5},{5,6},{6,7},{8,9},{9,10},{10,11},{11... | collective-permute-start | bytes 3145736 | tf_op jit(solution)/shard_map/while/body/eval_jaxpr/ppermute | solution.py:27
  221.6 2.4 collective-permute-done
  224.0 2.4 multiply_add_fusion.13
  226.4 14.3 %collective-permute-start = (f32[32,64,128]{2,1,0:T(8,128)}, f32[32,64,128]{2,1,0:T(8,128)S(1)}, u32[]{:S(2)}, u32[]{:S(2)}) collective-permute-start(f32[32,64,128]{2,1,0:T(8,128)} %multiply_add_fusion.13), channel_id=1, source_target_pairs={{0,1},{1,2},{2,3},{3,4},{4,5},{5,6},{6,7},{8,9},{9,10},{10,11},{11... | collective-permute-start | bytes 3145736 | tf_op jit(solution)/shard_map/while/body/eval_jaxpr/ppermute | solution.py:27
  240.8 2.4 collective-permute-done
  245.6 13.9 %collective-permute-start = (f32[32,64,128]{2,1,0:T(8,128)}, f32[32,64,128]{2,1,0:T(8,128)S(1)}, u32[]{:S(2)}, u32[]{:S(2)}) collective-permute-start(f32[32,64,128]{2,1,0:T(8,128)} %multiply_add_fusion.13), channel_id=1, source_target_pairs={{0,1},{1,2},{2,3},{3,4},{4,5},{5,6},{6,7},{8,9},{9,10},{10,11},{11... | collective-permute-start | bytes 3145736 | tf_op jit(solution)/shard_map/while/body/eval_jaxpr/ppermute | solution.py:27
  259.5 2.4 collective-permute-done
  264.3 13.9 %collective-permute-start = (f32[32,64,128]{2,1,0:T(8,128)}, f32[32,64,128]{2,1,0:T(8,128)S(1)}, u32[]{:S(2)}, u32[]{:S(2)}) collective-permute-start(f32[32,64,128]{2,1,0:T(8,128)} %multiply_add_fusion.13), channel_id=1, source_target_pairs={{0,1},{1,2},{2,3},{3,4},{4,5},{5,6},{6,7},{8,9},{9,10},{10,11},{11... | collective-permute-start | bytes 3145736 | tf_op jit(solution)/shard_map/while/body/eval_jaxpr/ppermute | solution.py:27
  278.2 2.4 collective-permute-done
  280.6 2.7 broadcast_multiply_fusion.1
  283.3 2.6 copy.205
  288.3 3.5 fusion.25
  291.8 2.5 copy.202
  294.3 3.4 multiply_reduce_fusion.13
  297.8 4.3 multiply_reduce_fusion.7
  302.2 4.2 multiply_reduce_fusion.6
  306.4 2.6 copy.207
  308.9 5.2 fusion.35
  317.0 2.9 multiply_reduce_fusion.8
  320.7 2.8 fusion.54
  323.6 134.3 %while.16 = (s32[]{:T(128)}, f32[32,64,128]{2,1,0:T(8,128)S(1)}, f32[1,32]{1,0:T(1,128)S(1)}, f32[32,64,128]{2,1,0:T(8,128)}, s32[]{:T(128)}, /*index=5*/s32[]{:T(128)}) while((s32[]{:T(128)}, f32[32,64,128]{2,1,0:T(8,128)S(1)}, f32[1,32]{1,0:T(1,128)S(1)}, f32[32,64,128]{2,1,0:T(8,128)}, s32[]{:T(128)}, ...), condition=%wide.region_8.9_spmd.clone, body=%wide.region_7.8_spmd.clone.sunk | while | flops 1310723 | bytes 6291703 | solution.py:222
  327.1 14.3 %collective-permute-done.1 = bf16[32,64,128]{2,1,0:T(8,128)(2,1)} collective-permute-done((bf16[32,64,128]{2,1,0:T(8,128)(2,1)}, bf16[32,64,128]{2,1,0:T(8,128)(2,1)}, u32[]{:S(2)}, u32[]{:S(2)}) %collective-permute-start.1) | collective-permute-done | bytes 524320 | tf_op jit(solution)/shard_map/while/body/eval_jaxpr/ppermute | solution.py:27
  346.0 10.2 %collective-permute-done.1 = bf16[32,64,128]{2,1,0:T(8,128)(2,1)} collective-permute-done((bf16[32,64,128]{2,1,0:T(8,128)(2,1)}, bf16[32,64,128]{2,1,0:T(8,128)(2,1)}, u32[]{:S(2)}, u32[]{:S(2)}) %collective-permute-start.1) | collective-permute-done | bytes 524320 | tf_op jit(solution)/shard_map/while/body/eval_jaxpr/ppermute | solution.py:27
  360.9 39.0 %collective-permute-done.1 = bf16[32,64,128]{2,1,0:T(8,128)(2,1)} collective-permute-done((bf16[32,64,128]{2,1,0:T(8,128)(2,1)}, bf16[32,64,128]{2,1,0:T(8,128)(2,1)}, u32[]{:S(2)}, u32[]{:S(2)}) %collective-permute-start.1) | collective-permute-done | bytes 524320 | tf_op jit(solution)/shard_map/while/body/eval_jaxpr/ppermute | solution.py:27
  404.5 9.5 %collective-permute-done.1 = bf16[32,64,128]{2,1,0:T(8,128)(2,1)} collective-permute-done((bf16[32,64,128]{2,1,0:T(8,128)(2,1)}, bf16[32,64,128]{2,1,0:T(8,128)(2,1)}, u32[]{:S(2)}, u32[]{:S(2)}) %collective-permute-start.1) | collective-permute-done | bytes 524320 | tf_op jit(solution)/shard_map/while/body/eval_jaxpr/ppermute | solution.py:27
  418.7 9.5 %collective-permute-done.1 = bf16[32,64,128]{2,1,0:T(8,128)(2,1)} collective-permute-done((bf16[32,64,128]{2,1,0:T(8,128)(2,1)}, bf16[32,64,128]{2,1,0:T(8,128)(2,1)}, u32[]{:S(2)}, u32[]{:S(2)}) %collective-permute-start.1) | collective-permute-done | bytes 524320 | tf_op jit(solution)/shard_map/while/body/eval_jaxpr/ppermute | solution.py:27
  432.8 9.5 %collective-permute-done.1 = bf16[32,64,128]{2,1,0:T(8,128)(2,1)} collective-permute-done((bf16[32,64,128]{2,1,0:T(8,128)(2,1)}, bf16[32,64,128]{2,1,0:T(8,128)(2,1)}, u32[]{:S(2)}, u32[]{:S(2)}) %collective-permute-start.1) | collective-permute-done | bytes 524320 | tf_op jit(solution)/shard_map/while/body/eval_jaxpr/ppermute | solution.py:27
  447.0 9.5 %collective-permute-done.1 = bf16[32,64,128]{2,1,0:T(8,128)(2,1)} collective-permute-done((bf16[32,64,128]{2,1,0:T(8,128)(2,1)}, bf16[32,64,128]{2,1,0:T(8,128)(2,1)}, u32[]{:S(2)}, u32[]{:S(2)}) %collective-permute-start.1) | collective-permute-done | bytes 524320 | tf_op jit(solution)/shard_map/while/body/eval_jaxpr/ppermute | solution.py:27
  457.9 3.3 fusion.36
  466.5 2.6 reduce_window_sum.41
  469.1 2.6 reduce_window_sum.42
  476.2 5.1 fusion.28
  481.3 2.6 copy.212
  483.9 2.5 copy.211
  486.4 3.5 fusion.120
  489.9 2.5 copy.209
  492.4 3.1 convolution_bitcast_fusion.1
  505.8 7.9 %collective-permute-done.3 = f32[3,2304]{1,0:T(4,128)S(1)} collective-permute-done((f32[3,2304]{1,0:T(4,128)S(1)}, f32[3,2304]{1,0:T(4,128)S(1)}, u32[]{:S(2)}, u32[]{:S(2)}) %collective-permute-start.3) | collective-permute-done | bytes 27680 | tf_op jit(solution)/shard_map/ppermute | solution.py:27
  514.9 2.9 copy.218
  517.9 3.9 copy.220
  522.0 3.9 fusion.9
  526.2 4.7 fusion.31
  530.9 78.9 %all-gather.13.cloned.1.call-done = bf16[1024,4384]{1,0:T(8,128)(2,1)} async-done(((bf16[128,4384]{1,0:T(8,128)(2,1)}), bf16[1024,4384]{1,0:T(8,128)(2,1)}) %all-gather.13.cloned.1.call-update) | async-done | bytes 8978448 | tf_op jit(solution)/shard_map/all_gather | solution.py:269
  609.9 6.0 fusion.4
  617.2 7.0 %multiply_reduce_fusion.14 = (f32[1024]{0:T(1024)S(1)}, f32[128]{0:T(128)S(1)}, f32[128,1024]{1,0:T(8,128)S(1)}) fusion(f32[1,128,1024]{2,1,0:T(8,128)S(1)} %copy-done.2, f32[128]{0:T(128)S(1)} %copy-done.78, f32[1024]{0:T(1024)S(1)} %slice.169, bf16[128,4384]{1,0:T(8,128)(2,1)S(1)} %copy-done.3, bf16[1024,4384]{1,0:T(8,128)(2,1)} %all-gather.7.cloned.1.call-done), kind=kOutput, calls=%fused_computation.102 | convolution fusion | flops 1150024576 | bytes 11158528 | tf_op jit(solution)/shard_map/dot_general | solution.py:249
  624.3 39.2 %psum.7 = f32[14688]{0:T(1024)S(1)} all-reduce(f32[14688]{0:T(1024)S(1)} %concatenate.23), channel_id=1, replica_groups=mesh['dp'=4,'seq'=8] {'dp','seq'}, use_global_device_ids=true, to_apply=%region_33.34 | all-reduce | flops 14688 | bytes 117504 | tf_op jit(solution)/shard_map/psum | solution.py:300
  668.5 2.4 divide_subtract_fusion
  (293 shorter events, 99.2 us)
Async XLA Ops:
  7.2 87.3 %all-gather.7.cloned.1.call-start = ((), (), s32[]{:S(2)}) async-start(), calls=%async_computation.2 | async-start | bytes 9461760 | tf_op jit(solution)/shard_map/all_gather | solution.py:153
  9.1 288.6 %all-gather.9.cloned.1.call-start = ((), (), s32[]{:S(2)}) async-start(), calls=%async_computation.3 | async-start | bytes 4325376 | tf_op jit(solution)/shard_map/all_gather | solution.py:154
  9.9 505.0 %all-gather.11.cloned.1.call-start = ((), (), s32[]{:S(2)}) async-start(), calls=%async_computation.4 | async-start | bytes 2359296 | tf_op jit(solution)/shard_map/all_gather | solution.py:268
  10.1 5.2 copy-start.81
  10.1 5.0 copy-start.77
  11.0 506.9 %all-gather.15.cloned.1.call-start = ((), (), s32[]{:S(2)}) async-start(), calls=%async_computation.6 | async-start | bytes 2359296 | tf_op jit(solution)/shard_map/all_gather | solution.py:270
  11.8 510.1 %all-gather.17.cloned.1.call-start = ((), (), s32[]{:S(2)}) async-start(), calls=%async_computation.7 | async-start | bytes 4718592 | tf_op jit(solution)/shard_map/all_gather | solution.py:271
  13.3 90.8 %copy-start.76 = (f32[32]{0:T(128)}, f32[32]{0:T(128)S(1)}, u32[]{:S(2)}) copy-start(f32[32]{0:T(128)S(1)} %get-tuple-element.499) | copy-start | bytes 388
  13.3 91.0 %copy-start.59 = (f32[32]{0:T(128)}, f32[32]{0:T(128)S(1)}, u32[]{:S(2)}) copy-start(f32[32]{0:T(128)S(1)} %get-tuple-element.498) | copy-start | bytes 388
  17.9 101.3 %copy-start.65 = (f32[128]{0:T(128)}, f32[128]{0:T(128)S(1)}, u32[]{:S(2)}) copy-start(f32[128]{0:T(128)S(1)} %get-tuple-element.509) | copy-start | bytes 1540
  99.6 16.0 %copy-start.6 = (f32[128,4384]{1,0:T(8,128)}, f32[128,4384]{1,0:T(8,128)S(1)}, u32[]{:S(2)}) copy-start(f32[128,4384]{1,0:T(8,128)S(1)} %get-tuple-element.518) | copy-start | bytes 6733828
  101.3 16.9 %collective-permute-start.2 = (bf16[3,2304]{1,0:T(4,128)(2,1)}, bf16[3,2304]{1,0:T(4,128)(2,1)}, u32[]{:S(2)}, u32[]{:S(2)}) collective-permute-start(bf16[3,2304]{1,0:T(4,128)(2,1)} %slice.205), channel_id=1, source_target_pairs={{0,1},{1,2},{2,3},{3,4},{4,5},{5,6},{6,7},{8,9},{9,10},{10,11},{11... | collective-permute-start | bytes 41480 | tf_op jit(solution)/shard_map/ppermute | solution.py:27
  108.6 212.0 %copy-start.27 = (f32[128,32]{0,1:T(8,128)}, f32[128,32]{0,1:T(8,128)S(1)}, u32[]{:S(2)}) copy-start(f32[128,32]{0,1:T(8,128)S(1)} %copy.204) | copy-start | bytes 49156
  110.8 7.4 %copy-start.47 = (f32[128,32]{0,1:T(8,128)}, f32[128,32]{0,1:T(8,128)S(1)}, u32[]{:S(2)}) copy-start(f32[128,32]{0,1:T(8,128)S(1)} %copy.201) | copy-start | bytes 49156
  130.9 5.0 collective-permute-start
  138.4 25.5 %collective-permute-start = (f32[32,64,128]{2,1,0:T(8,128)}, f32[32,64,128]{2,1,0:T(8,128)S(1)}, u32[]{:S(2)}, u32[]{:S(2)}) collective-permute-start(f32[32,64,128]{2,1,0:T(8,128)} %multiply_add_fusion.13), channel_id=1, source_target_pairs={{0,1},{1,2},{2,3},{3,4},{4,5},{5,6},{6,7},{8,9},{9,10},{10,11},{11... | collective-permute-start | bytes 3145736 | tf_op jit(solution)/shard_map/while/body/eval_jaxpr/ppermute | solution.py:27
  166.3 30.1 %collective-permute-start = (f32[32,64,128]{2,1,0:T(8,128)}, f32[32,64,128]{2,1,0:T(8,128)S(1)}, u32[]{:S(2)}, u32[]{:S(2)}) collective-permute-start(f32[32,64,128]{2,1,0:T(8,128)} %multiply_add_fusion.13), channel_id=1, source_target_pairs={{0,1},{1,2},{2,3},{3,4},{4,5},{5,6},{6,7},{8,9},{9,10},{10,11},{11... | collective-permute-start | bytes 3145736 | tf_op jit(solution)/shard_map/while/body/eval_jaxpr/ppermute | solution.py:27
  198.8 25.3 %collective-permute-start = (f32[32,64,128]{2,1,0:T(8,128)}, f32[32,64,128]{2,1,0:T(8,128)S(1)}, u32[]{:S(2)}, u32[]{:S(2)}) collective-permute-start(f32[32,64,128]{2,1,0:T(8,128)} %multiply_add_fusion.13), channel_id=1, source_target_pairs={{0,1},{1,2},{2,3},{3,4},{4,5},{5,6},{6,7},{8,9},{9,10},{10,11},{11... | collective-permute-start | bytes 3145736 | tf_op jit(solution)/shard_map/while/body/eval_jaxpr/ppermute | solution.py:27
  226.4 16.7 %collective-permute-start = (f32[32,64,128]{2,1,0:T(8,128)}, f32[32,64,128]{2,1,0:T(8,128)S(1)}, u32[]{:S(2)}, u32[]{:S(2)}) collective-permute-start(f32[32,64,128]{2,1,0:T(8,128)} %multiply_add_fusion.13), channel_id=1, source_target_pairs={{0,1},{1,2},{2,3},{3,4},{4,5},{5,6},{6,7},{8,9},{9,10},{10,11},{11... | collective-permute-start | bytes 3145736 | tf_op jit(solution)/shard_map/while/body/eval_jaxpr/ppermute | solution.py:27
  245.6 16.3 %collective-permute-start = (f32[32,64,128]{2,1,0:T(8,128)}, f32[32,64,128]{2,1,0:T(8,128)S(1)}, u32[]{:S(2)}, u32[]{:S(2)}) collective-permute-start(f32[32,64,128]{2,1,0:T(8,128)} %multiply_add_fusion.13), channel_id=1, source_target_pairs={{0,1},{1,2},{2,3},{3,4},{4,5},{5,6},{6,7},{8,9},{9,10},{10,11},{11... | collective-permute-start | bytes 3145736 | tf_op jit(solution)/shard_map/while/body/eval_jaxpr/ppermute | solution.py:27
  264.3 16.3 %collective-permute-start = (f32[32,64,128]{2,1,0:T(8,128)}, f32[32,64,128]{2,1,0:T(8,128)S(1)}, u32[]{:S(2)}, u32[]{:S(2)}) collective-permute-start(f32[32,64,128]{2,1,0:T(8,128)} %multiply_add_fusion.13), channel_id=1, source_target_pairs={{0,1},{1,2},{2,3},{3,4},{4,5},{5,6},{6,7},{8,9},{9,10},{10,11},{11... | collective-permute-start | bytes 3145736 | tf_op jit(solution)/shard_map/while/body/eval_jaxpr/ppermute | solution.py:27
  283.3 4.9 copy-start.48
  283.3 4.9 copy-start.61
  286.9 4.9 copy-start.50
  288.3 3.5 copy-start.14
  297.8 4.4 copy-start.5
  297.8 4.4 copy-start.7
  297.8 4.4 copy-start.8
  297.8 4.4 copy-start.9
  323.5 286.4 %all-gather.13.cloned.1.call-start = ((), (), s32[]{:S(2)}) async-start(), calls=%async_computation.5 | async-start | bytes 10321920 | tf_op jit(solution)/shard_map/all_gather | solution.py:269
  325.8 15.6 %collective-permute-start.1 = (bf16[32,64,128]{2,1,0:T(8,128)(2,1)}, bf16[32,64,128]{2,1,0:T(8,128)(2,1)}, u32[]{:S(2)}, u32[]{:S(2)}) collective-permute-start(bf16[32,64,128]{2,1,0:T(8,128)(2,1)} %fusion.145), channel_id=1, source_target_pairs={{1,0},{2,1},{3,2},{4,3},{5,4},{6,5},{7,6},{9,8},{10,9},{11,10},{12... | collective-permute-start | bytes 1572872 | tf_op jit(solution)/shard_map/while/body/eval_jaxpr/ppermute | solution.py:27
  344.7 11.4 %collective-permute-start.1 = (bf16[32,64,128]{2,1,0:T(8,128)(2,1)}, bf16[32,64,128]{2,1,0:T(8,128)(2,1)}, u32[]{:S(2)}, u32[]{:S(2)}) collective-permute-start(bf16[32,64,128]{2,1,0:T(8,128)(2,1)} %fusion.145), channel_id=1, source_target_pairs={{1,0},{2,1},{3,2},{4,3},{5,4},{6,5},{7,6},{9,8},{10,9},{11,10},{12... | collective-permute-start | bytes 1572872 | tf_op jit(solution)/shard_map/while/body/eval_jaxpr/ppermute | solution.py:27
  359.6 40.2 %collective-permute-start.1 = (bf16[32,64,128]{2,1,0:T(8,128)(2,1)}, bf16[32,64,128]{2,1,0:T(8,128)(2,1)}, u32[]{:S(2)}, u32[]{:S(2)}) collective-permute-start(bf16[32,64,128]{2,1,0:T(8,128)(2,1)} %fusion.145), channel_id=1, source_target_pairs={{1,0},{2,1},{3,2},{4,3},{5,4},{6,5},{7,6},{9,8},{10,9},{11,10},{12... | collective-permute-start | bytes 1572872 | tf_op jit(solution)/shard_map/while/body/eval_jaxpr/ppermute | solution.py:27
  403.2 10.8 %collective-permute-start.1 = (bf16[32,64,128]{2,1,0:T(8,128)(2,1)}, bf16[32,64,128]{2,1,0:T(8,128)(2,1)}, u32[]{:S(2)}, u32[]{:S(2)}) collective-permute-start(bf16[32,64,128]{2,1,0:T(8,128)(2,1)} %fusion.145), channel_id=1, source_target_pairs={{1,0},{2,1},{3,2},{4,3},{5,4},{6,5},{7,6},{9,8},{10,9},{11,10},{12... | collective-permute-start | bytes 1572872 | tf_op jit(solution)/shard_map/while/body/eval_jaxpr/ppermute | solution.py:27
  417.4 10.8 %collective-permute-start.1 = (bf16[32,64,128]{2,1,0:T(8,128)(2,1)}, bf16[32,64,128]{2,1,0:T(8,128)(2,1)}, u32[]{:S(2)}, u32[]{:S(2)}) collective-permute-start(bf16[32,64,128]{2,1,0:T(8,128)(2,1)} %fusion.145), channel_id=1, source_target_pairs={{1,0},{2,1},{3,2},{4,3},{5,4},{6,5},{7,6},{9,8},{10,9},{11,10},{12... | collective-permute-start | bytes 1572872 | tf_op jit(solution)/shard_map/while/body/eval_jaxpr/ppermute | solution.py:27
  431.6 10.8 %collective-permute-start.1 = (bf16[32,64,128]{2,1,0:T(8,128)(2,1)}, bf16[32,64,128]{2,1,0:T(8,128)(2,1)}, u32[]{:S(2)}, u32[]{:S(2)}) collective-permute-start(bf16[32,64,128]{2,1,0:T(8,128)(2,1)} %fusion.145), channel_id=1, source_target_pairs={{1,0},{2,1},{3,2},{4,3},{5,4},{6,5},{7,6},{9,8},{10,9},{11,10},{12... | collective-permute-start | bytes 1572872 | tf_op jit(solution)/shard_map/while/body/eval_jaxpr/ppermute | solution.py:27
  445.7 10.8 %collective-permute-start.1 = (bf16[32,64,128]{2,1,0:T(8,128)(2,1)}, bf16[32,64,128]{2,1,0:T(8,128)(2,1)}, u32[]{:S(2)}, u32[]{:S(2)}) collective-permute-start(bf16[32,64,128]{2,1,0:T(8,128)(2,1)} %fusion.145), channel_id=1, source_target_pairs={{1,0},{2,1},{3,2},{4,3},{5,4},{6,5},{7,6},{9,8},{10,9},{11,10},{12... | collective-permute-start | bytes 1572872 | tf_op jit(solution)/shard_map/while/body/eval_jaxpr/ppermute | solution.py:27
  489.9 5.7 copy-start.28
  497.4 4.1 copy-start.10
  497.5 4.1 copy-start.13
  497.5 4.1 copy-start.66
  497.5 4.1 copy-start.68
  497.5 4.1 copy-start.70
  503.9 9.8 %collective-permute-start.3 = (f32[3,2304]{1,0:T(4,128)S(1)}, f32[3,2304]{1,0:T(4,128)S(1)}, u32[]{:S(2)}, u32[]{:S(2)}) collective-permute-start(f32[3,2304]{1,0:T(4,128)S(1)} %pad_add_fusion.1), channel_id=1, source_target_pairs={{1,0},{2,1},{3,2},{4,3},{5,4},{6,5},{7,6},{9,8},{10,9},{11,10},{12... | collective-permute-start | bytes 82952 | tf_op jit(solution)/shard_map/ppermute | solution.py:27
  505.7 8.0 %copy-start.19 = (bf16[128,2048]{1,0:T(8,128)(2,1)S(1)}, bf16[128,2048]{1,0:T(8,128)(2,1)}, u32[]{:S(2)}) copy-start(bf16[128,2048]{1,0:T(8,128)(2,1)} %get-tuple-element.479) | copy-start | bytes 1572868
  505.8 8.0 %copy-start.37 = (bf16[128,32]{1,0:T(8,128)(2,1)S(1)}, bf16[128,32]{1,0:T(8,128)(2,1)}, u32[]{:S(2)}) copy-start(bf16[128,32]{1,0:T(8,128)(2,1)} %get-tuple-element.473) | copy-start | bytes 24580
  514.9 151.3 %reduce-scatter.9.cloned.1.call-start = ((), (), s32[]{:S(2)}) async-start(), calls=%async_computation.9 | async-start | bytes 655360
  517.8 4.0 copy-start.54
  517.8 4.0 copy-start.53
  517.8 4.0 copy-start.52
  521.9 4.1 copy-start.57
  521.9 4.2 copy-start.2
  522.0 4.2 copy-start.12
  525.9 142.6 %reduce-scatter.7.cloned.1.call-start = ((), (), s32[]{:S(2)}) async-start(), calls=%async_computation.8 | async-start | bytes 1433600
  609.9 6.1 copy-start.83
  609.9 6.2 copy-start.78
  617.2 7.0 %copy-start.55 = (f32[2304]{0:T(1024)S(1)}, f32[2304]{0:T(1024)}, u32[]{:S(2)}) copy-start(f32[2304]{0:T(1024)} %get-tuple-element.436) | copy-start | bytes 27652
  617.2 7.0 %copy-start.58 = (f32[2048]{0:T(1024)S(1)}, f32[2048]{0:T(1024)}, u32[]{:S(2)}) copy-start(f32[2048]{0:T(1024)} %get-tuple-element.434) | copy-start | bytes 24580
  617.2 7.0 %copy-start.80 = (f32[32]{0:T(128)S(1)}, f32[32]{0:T(128)}, u32[]{:S(2)}) copy-start(f32[32]{0:T(128)} %get-tuple-element.472) | copy-start | bytes 388
  617.2 46.3 %copy-start.82 = (f32[128]{0:T(128)S(1)}, f32[128]{0:T(128)}, u32[]{:S(2)}) copy-start(f32[128]{0:T(128)} %copy-done.81) | copy-start | bytes 1540
  617.2 46.3 %copy-start.21 = (f32[1,128,1024]{2,1,0:T(8,128)S(1)}, f32[1,128,1024]{2,1,0:T(8,128)}, u32[]{:S(2)}) copy-start(f32[1,128,1024]{2,1,0:T(8,128)} %param.17) | copy-start | bytes 1572868
  664.5 4.0 copy-start.18
  664.5 4.0 copy-start.24
  664.5 4.0 copy-start.25
  (44 other events, 83.5 us)
Sparse Core Ops, SparseCore 0:
  11.4 82.9 all-gather.6
  98.1 60.2 all-gather.8
  160.5 32.0 all-gather.10
  194.6 31.4 all-gather.14
  323.6 73.2 all-gather.16
  515.0 94.8 all-gather.12
  613.3 23.5 reduce-scatter.8
  639.7 28.6 reduce-scatter.6
where the time goes:
time: 686 us; the launch traced here: 678 us
  waiting for transfers between devices  282 us (41%)
  starting transfers between devices  132 us (19%)
  other arithmetic  89.3 us (13%)
  matrix products  67.5 us (10%)
  local copies, waits for them, and re-layouts  51.8 us (8%)
  blocking collectives  39.2 us (6%)
  between operations  15.4 us (2%)
    ppermute x16, starting transfers between devices, shifted_2(): return lax.ppermute(block, axis, route)  131 us
    ppermute x16, waiting for transfers between devices, shifted_2(): return lax.ppermute(block, axis, route)  126 us
    all_gather x1, waiting for transfers between devices, body(): proj_piece = lax.all_gather(grad_proj, 'seq', axis=0, tiled=True)  78.9 us
    all_gather x1, waiting for transfers between devices, body(): lax.all_gather(in_weight.astype(jnp.bfloat16), ('dp', 'seq'), axis=0, til...  76.6 us
    psum x1, blocking collectives, body(): vec_grad = lax.psum(vector, ('dp', 'seq'))  39.2 us
    add x7, other arithmetic, relay(): return shifted_2(decay[:, None, None] * entry_now + local_state, 'seq', 1)  16.8 us
    convert_element_type x7, other arithmetic, back_relay(): (own_part + decay[:, None, None] * later).astype(jnp.bfloat16)  15.5 us
    dot_general x3, matrix products, ssd_block(): inside = jnp.einsum('hij,jhp->ihp', mixing, values, precision=top_precision)  13.7 us
  transfers between devices with their start and end apart: 24, of which 18 were waited for; matrix products, arithmetic and copies ran while one was open for 30% of the time, Pallas kernels for 0%

commit v1 on v0

--- a/solution.py
+++ b/solution.py
@@ -297,7 +297,7 @@
     )
     in_grad = in_part.reshape(owner_rows, grad_proj.shape[1])
     out_grad = out_part.reshape(owner_rows, normed_out.shape[1])
-    vec_grad = lax.psum(vector, ("dp", "seq"))
+    vec_grad = jnp.sum(lax.all_gather(vector, ("dp", "seq")), axis=0)
     in_new, in_m_new, in_v_new = adamw_update(in_weight, in_grad, in_m, in_v)
     out_new, out_m_new, out_v_new = adamw_update(out_weight, out_grad, out_m, out_v)
     vec_new, vec_m_new, vec_v_new = adamw_update(vec_params, vec_grad, vec_m, vec_v)

time: 686 us -> 801 us (1.17)
  waiting for transfers between devices: 282 us -> 448 us
  blocking collectives: 39.2 us -> 0 us
  other arithmetic: 89.3 us -> 76.3 us
    unnamed x10 -> x12, waiting for transfers between devices: 0.41 us -> 179 us
    psum x1 -> x0, blocking collectives: 39.2 us -> none  [body(): vec_grad = lax.psum(vector, ('dp', 'seq'))]
    all_gather x1, starting transfers between devices: 0.04 us -> 12.5 us  [body(): proj_piece = lax.all_gather(grad_proj, 'seq', axis=0, tiled=True)]
    add x7, other arithmetic: 16.8 us -> 8.22 us  [relay(): return shifted_2(decay[:, None, None] * entry_now + local_state, 'seq', 1)]
    all_gather x1, waiting for transfers between devices: 78.9 us -> 70.4 us  [body(): proj_piece = lax.all_gather(grad_proj, 'seq', axis=0, tiled=True)]
  transfers between devices with their start and end apart: 24 -> 25, of which waited for: 18 -> 20; matrix products, arithmetic and copies ran while one was open for 30% -> 22% of each run, Pallas kernels for 0% -> 0%
where the time goes in v1:
time: 801 us; the launch traced here: 791 us
  waiting for transfers between devices  448 us (56%)
  starting transfers between devices  140 us (17%)
  other arithmetic  76.3 us (10%)
  matrix products  64.5 us (8%)
  local copies, waits for them, and re-layouts  45.9 us (6%)
  between operations  15.3 us (2%)
    unnamed x12, waiting for transfers between devices  179 us
    ppermute x16, starting transfers between devices, shifted_2(): return lax.ppermute(block, axis, route)  127 us
    ppermute x16, waiting for transfers between devices, shifted_2(): return lax.ppermute(block, axis, route)  121 us
    all_gather x1, waiting for transfers between devices, body(): lax.all_gather(in_weight.astype(jnp.bfloat16), ('dp', 'seq'), axis=0, til...  78 us
    all_gather x1, waiting for transfers between devices, body(): proj_piece = lax.all_gather(grad_proj, 'seq', axis=0, tiled=True)  70.4 us
  transfers between devices with their start and end apart: 25, of which 20 were waited for; matrix products, arithmetic and copies ran while one was open for 22% of the time, Pallas kernels for 0%

profile of v1, /device:TPU:0, one launch (start us, length us, event | category | flops | bytes accessed | tf_op | source)
XLA Modules:
  0.0 791.0 jit_solution(7889474800737952014)
XLA Ops:
  14.0 2.5 compare_convert_fusion
  16.6 78.0 %all-gather.8.cloned.1.call-done = bf16[1024,4384]{1,0:T(8,128)(2,1)} async-done(((bf16[32,4384]{1,0:T(8,128)(2,1)}), bf16[1024,4384]{1,0:T(8,128)(2,1)}) %all-gather.8.cloned.1.call-update) | async-done | bytes 8978448 | tf_op jit(solution)/shard_map/all_gather | solution.py:153
  94.5 5.0 fusion.124
  114.4 140.7 %while.7 = (s32[]{:T(128)}, f32[32,64,128]{2,1,0:T(8,128)S(1)}, f32[1,32]{1,0:T(1,128)S(1)}, f32[32,64,128]{2,1,0:T(8,128)S(1)}, s32[]{:T(128)}) while((s32[]{:T(128)}, f32[32,64,128]{2,1,0:T(8,128)S(1)}, f32[1,32]{1,0:T(1,128)S(1)}, f32[32,64,128]{2,1,0:T(8,128)S(1)}, s32[]{:T(128)}) %tuple.151), condition=%wide.region_3.4_spmd, body=%wide.region_2.3_spmd.sunk | while | flops 524290 | bytes 7340261 | solution.py:196
  115.6 3.2 collective-permute-start
  118.8 2.4 collective-permute-done
  122.4 17.4 %collective-permute-start = (f32[32,64,128]{2,1,0:T(8,128)}, f32[32,64,128]{2,1,0:T(8,128)S(1)}, u32[]{:S(2)}, u32[]{:S(2)}) collective-permute-start(f32[32,64,128]{2,1,0:T(8,128)} %multiply_add_fusion.13), channel_id=1, source_target_pairs={{0,1},{1,2},{2,3},{3,4},{4,5},{5,6},{6,7},{8,9},{9,10},{10,11},{11... | collective-permute-start | bytes 3145736 | tf_op jit(solution)/shard_map/while/body/eval_jaxpr/ppermute | solution.py:27
  139.8 3.0 collective-permute-done
  144.0 21.9 %collective-permute-start = (f32[32,64,128]{2,1,0:T(8,128)}, f32[32,64,128]{2,1,0:T(8,128)S(1)}, u32[]{:S(2)}, u32[]{:S(2)}) collective-permute-start(f32[32,64,128]{2,1,0:T(8,128)} %multiply_add_fusion.13), channel_id=1, source_target_pairs={{0,1},{1,2},{2,3},{3,4},{4,5},{5,6},{6,7},{8,9},{9,10},{10,11},{11... | collective-permute-start | bytes 3145736 | tf_op jit(solution)/shard_map/while/body/eval_jaxpr/ppermute | solution.py:27
  165.9 2.4 collective-permute-done
  169.5 30.7 %collective-permute-start = (f32[32,64,128]{2,1,0:T(8,128)}, f32[32,64,128]{2,1,0:T(8,128)S(1)}, u32[]{:S(2)}, u32[]{:S(2)}) collective-permute-start(f32[32,64,128]{2,1,0:T(8,128)} %multiply_add_fusion.13), channel_id=1, source_target_pairs={{0,1},{1,2},{2,3},{3,4},{4,5},{5,6},{6,7},{8,9},{9,10},{10,11},{11... | collective-permute-start | bytes 3145736 | tf_op jit(solution)/shard_map/while/body/eval_jaxpr/ppermute | solution.py:27
  200.3 2.4 collective-permute-done
  203.9 13.9 %collective-permute-start = (f32[32,64,128]{2,1,0:T(8,128)}, f32[32,64,128]{2,1,0:T(8,128)S(1)}, u32[]{:S(2)}, u32[]{:S(2)}) collective-permute-start(f32[32,64,128]{2,1,0:T(8,128)} %multiply_add_fusion.13), channel_id=1, source_target_pairs={{0,1},{1,2},{2,3},{3,4},{4,5},{5,6},{6,7},{8,9},{9,10},{10,11},{11... | collective-permute-start | bytes 3145736 | tf_op jit(solution)/shard_map/while/body/eval_jaxpr/ppermute | solution.py:27
  217.8 2.4 collective-permute-done
  221.3 13.9 %collective-permute-start = (f32[32,64,128]{2,1,0:T(8,128)}, f32[32,64,128]{2,1,0:T(8,128)S(1)}, u32[]{:S(2)}, u32[]{:S(2)}) collective-permute-start(f32[32,64,128]{2,1,0:T(8,128)} %multiply_add_fusion.13), channel_id=1, source_target_pairs={{0,1},{1,2},{2,3},{3,4},{4,5},{5,6},{6,7},{8,9},{9,10},{10,11},{11... | collective-permute-start | bytes 3145736 | tf_op jit(solution)/shard_map/while/body/eval_jaxpr/ppermute | solution.py:27
  235.3 2.4 collective-permute-done
  238.8 13.9 %collective-permute-start = (f32[32,64,128]{2,1,0:T(8,128)}, f32[32,64,128]{2,1,0:T(8,128)S(1)}, u32[]{:S(2)}, u32[]{:S(2)}) collective-permute-start(f32[32,64,128]{2,1,0:T(8,128)} %multiply_add_fusion.13), channel_id=1, source_target_pairs={{0,1},{1,2},{2,3},{3,4},{4,5},{5,6},{6,7},{8,9},{9,10},{10,11},{11... | collective-permute-start | bytes 3145736 | tf_op jit(solution)/shard_map/while/body/eval_jaxpr/ppermute | solution.py:27
  252.7 2.4 collective-permute-done
  255.2 2.7 broadcast_multiply_fusion.1
  257.8 2.6 copy.205
  261.3 3.4 fusion.25
  264.7 2.6 copy.202
  267.3 3.4 multiply_reduce_fusion.13
  270.7 4.3 multiply_reduce_fusion.7
  275.0 4.1 multiply_reduce_fusion.6
  279.7 12.5 %all-gather.14.cloned.1.call-start = ((), (), s32[]{:S(2)}) async-start(), calls=%async_computation.5 | async-start | bytes 10321920 | tf_op jit(solution)/shard_map/all_gather | solution.py:269
  293.3 2.6 copy.208
  295.9 2.6 copy.207
  298.5 2.9 fusion.54
  301.3 128.8 %while.16 = (s32[]{:T(128)}, f32[32,64,128]{2,1,0:T(8,128)S(1)}, f32[1,32]{1,0:T(1,128)S(1)}, f32[32,64,128]{2,1,0:T(8,128)}, s32[]{:T(128)}, /*index=5*/s32[]{:T(128)}) while((s32[]{:T(128)}, f32[32,64,128]{2,1,0:T(8,128)S(1)}, f32[1,32]{1,0:T(1,128)S(1)}, f32[32,64,128]{2,1,0:T(8,128)}, s32[]{:T(128)}, ...), condition=%wide.region_8.9_spmd.clone, body=%wide.region_7.8_spmd.clone.sunk | while | flops 1310723 | bytes 6291703 | solution.py:222
  301.3 2.3 fusion.145
  304.9 14.3 %collective-permute-done.1 = bf16[32,64,128]{2,1,0:T(8,128)(2,1)} collective-permute-done((bf16[32,64,128]{2,1,0:T(8,128)(2,1)}, bf16[32,64,128]{2,1,0:T(8,128)(2,1)}, u32[]{:S(2)}, u32[]{:S(2)}) %collective-permute-start.1) | collective-permute-done | bytes 524320 | tf_op jit(solution)/shard_map/while/body/eval_jaxpr/ppermute | solution.py:27
  320.4 2.3 fusion.145
  323.9 25.9 %collective-permute-done.1 = bf16[32,64,128]{2,1,0:T(8,128)(2,1)} collective-permute-done((bf16[32,64,128]{2,1,0:T(8,128)(2,1)}, bf16[32,64,128]{2,1,0:T(8,128)(2,1)}, u32[]{:S(2)}, u32[]{:S(2)}) %collective-permute-start.1) | collective-permute-done | bytes 524320 | tf_op jit(solution)/shard_map/while/body/eval_jaxpr/ppermute | solution.py:27
  354.5 10.5 %collective-permute-done.1 = bf16[32,64,128]{2,1,0:T(8,128)(2,1)} collective-permute-done((bf16[32,64,128]{2,1,0:T(8,128)(2,1)}, bf16[32,64,128]{2,1,0:T(8,128)(2,1)}, u32[]{:S(2)}, u32[]{:S(2)}) %collective-permute-start.1) | collective-permute-done | bytes 524320 | tf_op jit(solution)/shard_map/while/body/eval_jaxpr/ppermute | solution.py:27
  366.1 2.2 fusion.145
  369.6 16.8 %collective-permute-done.1 = bf16[32,64,128]{2,1,0:T(8,128)(2,1)} collective-permute-done((bf16[32,64,128]{2,1,0:T(8,128)(2,1)}, bf16[32,64,128]{2,1,0:T(8,128)(2,1)}, u32[]{:S(2)}, u32[]{:S(2)}) %collective-permute-start.1) | collective-permute-done | bytes 524320 | tf_op jit(solution)/shard_map/while/body/eval_jaxpr/ppermute | solution.py:27
  391.1 9.5 %collective-permute-done.1 = bf16[32,64,128]{2,1,0:T(8,128)(2,1)} collective-permute-done((bf16[32,64,128]{2,1,0:T(8,128)(2,1)}, bf16[32,64,128]{2,1,0:T(8,128)(2,1)}, u32[]{:S(2)}, u32[]{:S(2)}) %collective-permute-start.1) | collective-permute-done | bytes 524320 | tf_op jit(solution)/shard_map/while/body/eval_jaxpr/ppermute | solution.py:27
  405.3 9.5 %collective-permute-done.1 = bf16[32,64,128]{2,1,0:T(8,128)(2,1)} collective-permute-done((bf16[32,64,128]{2,1,0:T(8,128)(2,1)}, bf16[32,64,128]{2,1,0:T(8,128)(2,1)}, u32[]{:S(2)}, u32[]{:S(2)}) %collective-permute-start.1) | collective-permute-done | bytes 524320 | tf_op jit(solution)/shard_map/while/body/eval_jaxpr/ppermute | solution.py:27
  419.5 9.5 %collective-permute-done.1 = bf16[32,64,128]{2,1,0:T(8,128)(2,1)} collective-permute-done((bf16[32,64,128]{2,1,0:T(8,128)(2,1)}, bf16[32,64,128]{2,1,0:T(8,128)(2,1)}, u32[]{:S(2)}, u32[]{:S(2)}) %collective-permute-start.1) | collective-permute-done | bytes 524320 | tf_op jit(solution)/shard_map/while/body/eval_jaxpr/ppermute | solution.py:27
  431.2 3.1 fusion.36
  434.3 2.5 convolution_bitcast_fusion.2
  436.8 4.2 fusion.35
  442.4 2.6 multiply_reduce_fusion.8
  450.7 2.6 reduce_window_sum.41
  453.3 2.6 reduce_window_sum.42
  457.3 2.3 fusion.116
  460.5 4.8 fusion.28
  465.3 2.7 copy.212
  469.3 3.8 convolution_bitcast_fusion
  473.1 2.5 fusion.120
  485.1 7.9 collective-permute-done.3
  495.2 7.2 multiply_reduce_fusion.14
  504.7 2.9 copy.220
  507.7 3.7 fusion.9
  511.5 2.9 copy.218
  514.4 70.4 %all-gather.14.cloned.1.call-done = bf16[1024,4384]{1,0:T(8,128)(2,1)} async-done(((bf16[128,4384]{1,0:T(8,128)(2,1)}), bf16[1024,4384]{1,0:T(8,128)(2,1)}) %all-gather.14.cloned.1.call-update) | async-done | bytes 8978448 | tf_op jit(solution)/shard_map/all_gather | solution.py:269
  584.8 6.0 fusion.4
  591.9 4.6 fusion.31
  597.5 124.4 %all-reduce.21.cloned.1.call-done = f32[470016]{0:T(1024)} async-done(((f32[470016]{0:T(1024)}), f32[470016]{0:T(1024)}) %all-reduce.21.cloned.1.call-update) | async-done | bytes 1880080
  721.9 2.6 reshape.669
  726.1 24.1 %reduce-scatter.9.cloned.1.call-done = bf16[1,32,2048]{2,1,0:T(8,128)(2,1)} async-done(((bf16[4,32,2048]{2,1,0:T(8,128)(2,1)}), bf16[1,32,2048]{2,1,0:T(8,128)(2,1)}) %reduce-scatter.9.cloned.1.call-update) | async-done | bytes 131088
  752.1 29.5 %reduce-scatter.7.cloned.1.call-done = bf16[1,32,4384]{2,1,0:T(8,128)(2,1)} async-done(((bf16[4,32,4384]{2,1,0:T(8,128)(2,1)}), bf16[1,32,4384]{2,1,0:T(8,128)(2,1)}) %reduce-scatter.7.cloned.1.call-update) | async-done | bytes 280592
  781.6 2.4 divide_subtract_fusion
  (299 shorter events, 88.9 us)
Async XLA Ops:
  7.2 87.3 %all-gather.8.cloned.1.call-start = ((), (), s32[]{:S(2)}) async-start(), calls=%async_computation.2 | async-start | bytes 9461760 | tf_op jit(solution)/shard_map/all_gather | solution.py:153
  9.1 261.5 %all-gather.10.cloned.1.call-start = ((), (), s32[]{:S(2)}) async-start(), calls=%async_computation.3 | async-start | bytes 4325376 | tf_op jit(solution)/shard_map/all_gather | solution.py:154
  9.9 494.8 %all-gather.16.cloned.1.call-start = ((), (), s32[]{:S(2)}) async-start(), calls=%async_computation.6 | async-start | bytes 2359296 | tf_op jit(solution)/shard_map/all_gather | solution.py:270
  10.7 497.0 %all-gather.18.cloned.1.call-start = ((), (), s32[]{:S(2)}) async-start(), calls=%async_computation.7 | async-start | bytes 4718592 | tf_op jit(solution)/shard_map/all_gather | solution.py:271
  10.8 97.6 %copy-start.39 = (f32[2304]{0:T(1024)}, f32[2304]{0:T(1024)S(1)}, u32[]{:S(2)}) copy-start(f32[2304]{0:T(1024)S(1)} %get-tuple-element.501) | copy-start | bytes 27652
  10.8 97.6 %copy-start.41 = (f32[2304]{0:T(1024)}, f32[2304]{0:T(1024)S(1)}, u32[]{:S(2)}) copy-start(f32[2304]{0:T(1024)S(1)} %get-tuple-element.502) | copy-start | bytes 27652
  10.8 97.6 %copy-start.43 = (f32[2304]{0:T(1024)}, f32[2304]{0:T(1024)S(1)}, u32[]{:S(2)}) copy-start(f32[2304]{0:T(1024)S(1)} %get-tuple-element.503) | copy-start | bytes 27652
  10.8 97.6 %copy-start.45 = (f32[2304]{0:T(1024)}, f32[2304]{0:T(1024)S(1)}, u32[]{:S(2)}) copy-start(f32[2304]{0:T(1024)S(1)} %get-tuple-element.504) | copy-start | bytes 27652
  11.7 91.1 %copy-start.75 = (f32[32]{0:T(128)}, f32[32]{0:T(128)S(1)}, u32[]{:S(2)}) copy-start(f32[32]{0:T(128)S(1)} %get-tuple-element.499) | copy-start | bytes 388
  11.7 91.3 %copy-start.59 = (f32[32]{0:T(128)}, f32[32]{0:T(128)S(1)}, u32[]{:S(2)}) copy-start(f32[32]{0:T(128)S(1)} %get-tuple-element.498) | copy-start | bytes 388
  14.0 85.6 %copy-start.19 = (bf16[128,1024]{1,0:T(8,128)(2,1)}, bf16[128,1024]{1,0:T(8,128)(2,1)S(1)}, u32[]{:S(2)}) copy-start(bf16[128,1024]{1,0:T(8,128)(2,1)S(1)} %multiply_convert_fusion.2) | copy-start | bytes 786436
  16.6 86.5 %copy-start.73 = (f32[128]{0:T(128)}, f32[128]{0:T(128)S(1)}, u32[]{:S(2)}) copy-start(f32[128]{0:T(128)S(1)} %get-tuple-element.506) | copy-start | bytes 1540
  16.6 86.5 %copy-start.74 = (f32[128]{0:T(128)}, f32[128]{0:T(128)S(1)}, u32[]{:S(2)}) copy-start(f32[128]{0:T(128)S(1)} %get-tuple-element.507) | copy-start | bytes 1540
  16.6 91.8 %copy-start.66 = (f32[128]{0:T(128)}, f32[128]{0:T(128)S(1)}, u32[]{:S(2)}) copy-start(f32[128]{0:T(128)S(1)} %get-tuple-element.509) | copy-start | bytes 1540
  16.6 91.9 %copy-start.68 = (f32[128]{0:T(128)}, f32[128]{0:T(128)S(1)}, u32[]{:S(2)}) copy-start(f32[128]{0:T(128)S(1)} %get-tuple-element.510) | copy-start | bytes 1540
  16.6 91.9 %copy-start.70 = (f32[128]{0:T(128)}, f32[128]{0:T(128)S(1)}, u32[]{:S(2)}) copy-start(f32[128]{0:T(128)S(1)} %get-tuple-element.511) | copy-start | bytes 1540
  99.6 8.5 %copy-start.6 = (f32[128,4384]{1,0:T(8,128)}, f32[128,4384]{1,0:T(8,128)S(1)}, u32[]{:S(2)}) copy-start(f32[128,4384]{1,0:T(8,128)S(1)} %get-tuple-element.518) | copy-start | bytes 6733828
  100.6 7.5 collective-permute-start.2
  103.0 5.3 copy-start.72
  104.8 150.3 %copy-start.31 = (f32[128,32]{0,1:T(8,128)}, f32[128,32]{0,1:T(8,128)S(1)}, u32[]{:S(2)}) copy-start(f32[128,32]{0,1:T(8,128)S(1)} %copy.204) | copy-start | bytes 49156
  115.6 5.6 collective-permute-start
  122.4 20.4 %collective-permute-start = (f32[32,64,128]{2,1,0:T(8,128)}, f32[32,64,128]{2,1,0:T(8,128)S(1)}, u32[]{:S(2)}, u32[]{:S(2)}) collective-permute-start(f32[32,64,128]{2,1,0:T(8,128)} %multiply_add_fusion.13), channel_id=1, source_target_pairs={{0,1},{1,2},{2,3},{3,4},{4,5},{5,6},{6,7},{8,9},{9,10},{10,11},{11... | collective-permute-start | bytes 3145736 | tf_op jit(solution)/shard_map/while/body/eval_jaxpr/ppermute | solution.py:27
  144.0 24.3 %collective-permute-start = (f32[32,64,128]{2,1,0:T(8,128)}, f32[32,64,128]{2,1,0:T(8,128)S(1)}, u32[]{:S(2)}, u32[]{:S(2)}) collective-permute-start(f32[32,64,128]{2,1,0:T(8,128)} %multiply_add_fusion.13), channel_id=1, source_target_pairs={{0,1},{1,2},{2,3},{3,4},{4,5},{5,6},{6,7},{8,9},{9,10},{10,11},{11... | collective-permute-start | bytes 3145736 | tf_op jit(solution)/shard_map/while/body/eval_jaxpr/ppermute | solution.py:27
  169.5 33.2 %collective-permute-start = (f32[32,64,128]{2,1,0:T(8,128)}, f32[32,64,128]{2,1,0:T(8,128)S(1)}, u32[]{:S(2)}, u32[]{:S(2)}) collective-permute-start(f32[32,64,128]{2,1,0:T(8,128)} %multiply_add_fusion.13), channel_id=1, source_target_pairs={{0,1},{1,2},{2,3},{3,4},{4,5},{5,6},{6,7},{8,9},{9,10},{10,11},{11... | collective-permute-start | bytes 3145736 | tf_op jit(solution)/shard_map/while/body/eval_jaxpr/ppermute | solution.py:27
  203.9 16.3 %collective-permute-start = (f32[32,64,128]{2,1,0:T(8,128)}, f32[32,64,128]{2,1,0:T(8,128)S(1)}, u32[]{:S(2)}, u32[]{:S(2)}) collective-permute-start(f32[32,64,128]{2,1,0:T(8,128)} %multiply_add_fusion.13), channel_id=1, source_target_pairs={{0,1},{1,2},{2,3},{3,4},{4,5},{5,6},{6,7},{8,9},{9,10},{10,11},{11... | collective-permute-start | bytes 3145736 | tf_op jit(solution)/shard_map/while/body/eval_jaxpr/ppermute | solution.py:27
  221.3 16.3 %collective-permute-start = (f32[32,64,128]{2,1,0:T(8,128)}, f32[32,64,128]{2,1,0:T(8,128)S(1)}, u32[]{:S(2)}, u32[]{:S(2)}) collective-permute-start(f32[32,64,128]{2,1,0:T(8,128)} %multiply_add_fusion.13), channel_id=1, source_target_pairs={{0,1},{1,2},{2,3},{3,4},{4,5},{5,6},{6,7},{8,9},{9,10},{10,11},{11... | collective-permute-start | bytes 3145736 | tf_op jit(solution)/shard_map/while/body/eval_jaxpr/ppermute | solution.py:27
  238.8 16.3 %collective-permute-start = (f32[32,64,128]{2,1,0:T(8,128)}, f32[32,64,128]{2,1,0:T(8,128)S(1)}, u32[]{:S(2)}, u32[]{:S(2)}) collective-permute-start(f32[32,64,128]{2,1,0:T(8,128)} %multiply_add_fusion.13), channel_id=1, source_target_pairs={{0,1},{1,2},{2,3},{3,4},{4,5},{5,6},{6,7},{8,9},{9,10},{10,11},{11... | collective-permute-start | bytes 3145736 | tf_op jit(solution)/shard_map/while/body/eval_jaxpr/ppermute | solution.py:27
  260.6 4.1 copy-start.51
  270.7 4.3 copy-start.8
  270.7 4.3 copy-start.9
  270.7 4.3 copy-start.10
  275.0 17.3 %copy-start.49 = (f32[128,32]{0,1:T(8,128)S(1)}, f32[128,32]{0,1:T(8,128)}, u32[]{:S(2)}) copy-start(f32[128,32]{0,1:T(8,128)} %copy.201) | copy-start | bytes 49156
  279.1 232.4 %all-gather.12.cloned.1.call-start = ((), (), s32[]{:S(2)}) async-start(), calls=%async_computation.4 | async-start | bytes 2359296 | tf_op jit(solution)/shard_map/all_gather | solution.py:268
  279.7 305.1 %all-gather.14.cloned.1.call-start = ((), (), s32[]{:S(2)}) async-start(), calls=%async_computation.5 | async-start | bytes 10321920 | tf_op jit(solution)/shard_map/all_gather | solution.py:269
  303.6 15.6 %collective-permute-start.1 = (bf16[32,64,128]{2,1,0:T(8,128)(2,1)}, bf16[32,64,128]{2,1,0:T(8,128)(2,1)}, u32[]{:S(2)}, u32[]{:S(2)}) collective-permute-start(bf16[32,64,128]{2,1,0:T(8,128)(2,1)} %fusion.145), channel_id=1, source_target_pairs={{1,0},{2,1},{3,2},{4,3},{5,4},{6,5},{7,6},{9,8},{10,9},{11,10},{12... | collective-permute-start | bytes 1572872 | tf_op jit(solution)/shard_map/while/body/eval_jaxpr/ppermute | solution.py:27
  322.6 27.1 %collective-permute-start.1 = (bf16[32,64,128]{2,1,0:T(8,128)(2,1)}, bf16[32,64,128]{2,1,0:T(8,128)(2,1)}, u32[]{:S(2)}, u32[]{:S(2)}) collective-permute-start(bf16[32,64,128]{2,1,0:T(8,128)(2,1)} %fusion.145), channel_id=1, source_target_pairs={{1,0},{2,1},{3,2},{4,3},{5,4},{6,5},{7,6},{9,8},{10,9},{11,10},{12... | collective-permute-start | bytes 1572872 | tf_op jit(solution)/shard_map/while/body/eval_jaxpr/ppermute | solution.py:27
  353.2 11.8 %collective-permute-start.1 = (bf16[32,64,128]{2,1,0:T(8,128)(2,1)}, bf16[32,64,128]{2,1,0:T(8,128)(2,1)}, u32[]{:S(2)}, u32[]{:S(2)}) collective-permute-start(bf16[32,64,128]{2,1,0:T(8,128)(2,1)} %fusion.145), channel_id=1, source_target_pairs={{1,0},{2,1},{3,2},{4,3},{5,4},{6,5},{7,6},{9,8},{10,9},{11,10},{12... | collective-permute-start | bytes 1572872 | tf_op jit(solution)/shard_map/while/body/eval_jaxpr/ppermute | solution.py:27
  368.3 18.1 %collective-permute-start.1 = (bf16[32,64,128]{2,1,0:T(8,128)(2,1)}, bf16[32,64,128]{2,1,0:T(8,128)(2,1)}, u32[]{:S(2)}, u32[]{:S(2)}) collective-permute-start(bf16[32,64,128]{2,1,0:T(8,128)(2,1)} %fusion.145), channel_id=1, source_target_pairs={{1,0},{2,1},{3,2},{4,3},{5,4},{6,5},{7,6},{9,8},{10,9},{11,10},{12... | collective-permute-start | bytes 1572872 | tf_op jit(solution)/shard_map/while/body/eval_jaxpr/ppermute | solution.py:27
  389.8 10.8 %collective-permute-start.1 = (bf16[32,64,128]{2,1,0:T(8,128)(2,1)}, bf16[32,64,128]{2,1,0:T(8,128)(2,1)}, u32[]{:S(2)}, u32[]{:S(2)}) collective-permute-start(bf16[32,64,128]{2,1,0:T(8,128)(2,1)} %fusion.145), channel_id=1, source_target_pairs={{1,0},{2,1},{3,2},{4,3},{5,4},{6,5},{7,6},{9,8},{10,9},{11,10},{12... | collective-permute-start | bytes 1572872 | tf_op jit(solution)/shard_map/while/body/eval_jaxpr/ppermute | solution.py:27
  404.0 10.8 %collective-permute-start.1 = (bf16[32,64,128]{2,1,0:T(8,128)(2,1)}, bf16[32,64,128]{2,1,0:T(8,128)(2,1)}, u32[]{:S(2)}, u32[]{:S(2)}) collective-permute-start(bf16[32,64,128]{2,1,0:T(8,128)(2,1)} %fusion.145), channel_id=1, source_target_pairs={{1,0},{2,1},{3,2},{4,3},{5,4},{6,5},{7,6},{9,8},{10,9},{11,10},{12... | collective-permute-start | bytes 1572872 | tf_op jit(solution)/shard_map/while/body/eval_jaxpr/ppermute | solution.py:27
  418.2 10.8 %collective-permute-start.1 = (bf16[32,64,128]{2,1,0:T(8,128)(2,1)}, bf16[32,64,128]{2,1,0:T(8,128)(2,1)}, u32[]{:S(2)}, u32[]{:S(2)}) collective-permute-start(bf16[32,64,128]{2,1,0:T(8,128)(2,1)} %fusion.145), channel_id=1, source_target_pairs={{1,0},{2,1},{3,2},{4,3},{5,4},{6,5},{7,6},{9,8},{10,9},{11,10},{12... | collective-permute-start | bytes 1572872 | tf_op jit(solution)/shard_map/while/body/eval_jaxpr/ppermute | solution.py:27
  436.8 5.7 copy-start.1
  477.1 4.0 copy-start.12
  477.1 4.0 copy-start.33
  477.2 4.0 copy-start.67
  477.2 4.0 copy-start.69
  477.2 4.0 copy-start.71
  483.2 9.8 %collective-permute-start.3 = (f32[3,2304]{1,0:T(4,128)S(1)}, f32[3,2304]{1,0:T(4,128)S(1)}, u32[]{:S(2)}, u32[]{:S(2)}) collective-permute-start(f32[3,2304]{1,0:T(4,128)S(1)} %pad_add_fusion.1), channel_id=1, source_target_pairs={{1,0},{2,1},{3,2},{4,3},{5,4},{6,5},{7,6},{9,8},{10,9},{11,10},{12... | collective-permute-start | bytes 82952 | tf_op jit(solution)/shard_map/ppermute | solution.py:27
  485.0 8.0 %copy-start.23 = (bf16[128,2048]{1,0:T(8,128)(2,1)S(1)}, bf16[128,2048]{1,0:T(8,128)(2,1)}, u32[]{:S(2)}) copy-start(bf16[128,2048]{1,0:T(8,128)(2,1)} %get-tuple-element.479) | copy-start | bytes 1572868
  485.0 8.0 %copy-start.38 = (bf16[128,32]{1,0:T(8,128)(2,1)S(1)}, bf16[128,32]{1,0:T(8,128)(2,1)}, u32[]{:S(2)}) copy-start(bf16[128,32]{1,0:T(8,128)(2,1)} %get-tuple-element.473) | copy-start | bytes 24580
  494.2 227.7 %all-reduce.21.cloned.1.call-start = ((), (), s32[]{:S(2)}) async-start(), calls=%async_computation.8 | async-start | bytes 3760128
  495.2 7.2 copy-start.58
  495.2 7.2 copy-start.79
  504.6 245.5 %reduce-scatter.9.cloned.1.call-start = ((), (), s32[]{:S(2)}) async-start(), calls=%async_computation.10 | async-start | bytes 655360
  511.4 270.2 %reduce-scatter.7.cloned.1.call-start = ((), (), s32[]{:S(2)}) async-start(), calls=%async_computation.9 | async-start | bytes 1433600
  591.9 4.6 copy-start.81
  591.9 4.6 copy-start.25
  724.6 25.6 %copy-start.27 = (f32[32,2048]{1,0:T(8,128)S(1)}, f32[32,2048]{1,0:T(8,128)}, u32[]{:S(2)}) copy-start(f32[32,2048]{1,0:T(8,128)} %param.20) | copy-start | bytes 786436
  724.6 25.6 %copy-start.34 = (f32[32,2048]{1,0:T(8,128)S(1)}, f32[32,2048]{1,0:T(8,128)}, u32[]{:S(2)}) copy-start(f32[32,2048]{1,0:T(8,128)} %param.23) | copy-start | bytes 786436
  724.6 25.6 %copy-start.35 = (f32[32,2048]{1,0:T(8,128)S(1)}, f32[32,2048]{1,0:T(8,128)}, u32[]{:S(2)}) copy-start(f32[32,2048]{1,0:T(8,128)} %param.24) | copy-start | bytes 786436
  725.4 26.7 %copy-start.37 = (f32[14688]{0:T(1024)}, f32[14688]{0:T(1024)S(1)}, u32[]{:S(2)}) copy-start(f32[14688]{0:T(1024)S(1)} %reduce_sum.303) | copy-start | bytes 176260
  725.4 56.2 %copy-start.22 = (f32[32,4384]{1,0:T(8,128)S(1)}, f32[32,4384]{1,0:T(8,128)}, u32[]{:S(2)}) copy-start(f32[32,4384]{1,0:T(8,128)} %param.19) | copy-start | bytes 1683460
  725.4 56.2 %copy-start.28 = (f32[32,4384]{1,0:T(8,128)S(1)}, f32[32,4384]{1,0:T(8,128)}, u32[]{:S(2)}) copy-start(f32[32,4384]{1,0:T(8,128)} %param.21) | copy-start | bytes 1683460
  725.4 56.2 %copy-start.29 = (f32[32,4384]{1,0:T(8,128)S(1)}, f32[32,4384]{1,0:T(8,128)}, u32[]{:S(2)}) copy-start(f32[32,4384]{1,0:T(8,128)} %param.22) | copy-start | bytes 1683460
  (45 other events, 90.8 us)
Sparse Core Ops, SparseCore 0:
  11.4 83.0 all-gather.7
  98.1 60.4 all-gather.9
  160.8 33.7 all-gather.15
  279.3 63.3 all-gather.17
  344.7 33.5 all-gather.11
  494.3 90.4 all-gather.13
  590.2 131.6 all-reduce.20
  725.3 24.8 reduce-scatter.8
  753.1 28.4 reduce-scatter.6
